TPU v7x, 128 devices: a whole 4x4x4 slice. The times are simulated.
128 devices in a mesh: src: 8 (over z, core), rcv: 16 (over y, x).
Axes of the slice: x: 4, y: 4, z: 4, core: 2. Of those that a mesh axis runs over, the one named last changes fastest.
Arguments:
- data: bfloat16 [2, 16384, 16384], P(None, 'src', 'rcv'), may hold values from -15 to 15
- observed: int32 [256, 256], P('src', 'rcv'), may hold values 0 or 1
- band_width: int32 [1], replicated, may hold values from 24 to 48
- left_factor: float32 [32, 8, 64, 256], P(None, 'src'), may hold values from -1.5 to 1.5
- right_factor: float32 [6, 16, 64, 256], P(None, 'rcv'), may hold values from -1.5 to 1.5
Outputs:
- left_out: float32 [32, 8, 64, 256], P(None, 'src')
- right_out: float32 [6, 16, 64, 256], P(None, 'rcv')
All inputs are finite; a program needn't handle non-finite values. No bound on the sum of `observed` on one device may be relied on, other than what follows from the above.
Results may differ from a plain program's by a relative error of at most 0.0044.
The roundings to bfloat16 on the way count: a program that leaves them out, or rounds other values in their place, can miss the bound.
Values may be sent and summed in bfloat16 or wider, within the bound.
No kernel may reach another device: no remote copies, remote signals or barrier semaphores. Data moves between devices by JAX's collectives and lax.ppermute only.
A program may use at most 128 MiB of HBM per device.

v0:
```python
import jax
import jax.numpy as jnp
from jax import lax
from jax.sharding import PartitionSpec as P

ITERS = 2
epsilon = 1e-06


def stacked(factor):
    half_width = factor.shape[1] // 2
    turned = jnp.concatenate([-factor[:, half_width:], factor[:, :half_width]], axis=1)
    return jnp.concatenate([factor, turned], axis=0)


def times_t(first, second):
    return lax.dot_general(
        first, second, (((1,), (1,)), ((), ())), preferred_element_type=jnp.float32
    )


def combine(products):
    count = products.shape[0] // 2
    half_width = products.shape[1] // 2
    upper_part = products[:count]
    lower_part = products[count:]
    return jnp.concatenate(
        [
            upper_part[:, :half_width] + lower_part[:, half_width:],
            upper_part[:, half_width:] - lower_part[:, :half_width],
        ],
        axis=1,
    )


def left_sums(own_rows, curvature):
    numerator, denominator = lax.psum(
        (jnp.sum(own_rows * own_rows), jnp.sum(curvature * curvature)), ("src", "rcv")
    )
    return numerator / (denominator + epsilon)


def right_sums(own_rows, curvature):
    numerator, denominator = lax.psum(
        (jnp.sum(own_rows * own_rows), jnp.sum(curvature * curvature)), ("src", "rcv")
    )
    return numerator / (denominator + epsilon)


def per_device(data, observed, band_width, left_factor, right_factor):
    src_index = lax.axis_index("src")
    rcv_index = lax.axis_index("rcv")
    src_count = lax.axis_size("src")
    rcv_count = lax.axis_size("rcv")
    src_blocks, rcv_blocks = observed.shape
    block_edge = data.shape[1] // src_blocks
    offset_slots = right_factor.shape[0]
    factor_width = left_factor.shape[3]
    per_peer = rcv_blocks // rcv_count
    half_slots = offset_slots // 2
    source_rows = src_index * src_blocks + jnp.arange(src_blocks, dtype=jnp.int32)
    destinations = jnp.arange(rcv_count, dtype=jnp.int32)
    group_ids = jnp.arange(per_peer, dtype=jnp.int32)
    wanted = (
        destinations[None, :, None] + source_rows[:, None, None]
    ) % rcv_count + rcv_count * group_ids[None, None, :]
    selector = (
        jnp.arange(rcv_blocks, dtype=jnp.int32)[None, None, None, :] == wanted[..., None]
    ).astype(jnp.bfloat16)
    blocked = data.reshape(2, src_blocks, block_edge, rcv_blocks, block_edge)
    outgoing = jnp.einsum(
        "ripjq,idgj->drigpq", blocked, selector, preferred_element_type=jnp.float32
    ).astype(jnp.bfloat16)
    out_flags = jnp.einsum(
        "ij,idgj->dig", observed.astype(jnp.bfloat16), selector, preferred_element_type=jnp.float32
    )
    out_flags = out_flags.astype(jnp.bfloat16).reshape(rcv_count, 1, src_blocks, per_peer, 1, 1)
    arrived, arrived_flags = (
        lax.all_to_all(outgoing, "rcv", split_axis=0, concat_axis=0, tiled=True),
        lax.all_to_all(out_flags, "rcv", split_axis=0, concat_axis=0, tiled=True),
    )
    slot_ids = jnp.arange(offset_slots, dtype=jnp.int32)
    source_key = (
        slot_ids[None, :] - half_slots + (rcv_index + source_rows[:, None]) // rcv_count
    ) % (rcv_count * per_peer)
    source_keys = jnp.arange(rcv_count, dtype=jnp.int32)[:, None] * per_peer + group_ids[None, :]
    chooser = (source_keys[None, None, :, :] == source_key[:, :, None, None]).astype(jnp.bfloat16)
    sheared = jnp.einsum(
        "brigpq,itbg->riptq", arrived, chooser, preferred_element_type=jnp.float32
    ).astype(jnp.bfloat16)
    shear_flags = jnp.einsum(
        "big,itbg->it",
        arrived_flags.reshape(rcv_count, src_blocks, per_peer),
        chooser,
        preferred_element_type=jnp.float32,
    ).astype(jnp.bfloat16)
    per_dest = src_blocks // src_count
    offsets = rcv_count * slot_ids + rcv_index - offset_slots * rcv_count // 2
    shifts = offsets // 2
    targets = jnp.arange(src_count, dtype=jnp.int32)
    row_pick = (targets[:, None] - shifts[None, :]) % src_count
    selector_two = (
        jnp.arange(src_count, dtype=jnp.int32)[None, None, :] == row_pick[:, :, None]
    ).astype(jnp.bfloat16)
    split_rows = sheared.reshape(2, per_dest, src_count, block_edge, offset_slots, block_edge)
    outgoing_two = jnp.einsum(
        "ruvptq,etv->eruptq", split_rows, selector_two, preferred_element_type=jnp.float32
    ).astype(jnp.bfloat16)
    flags_two = jnp.einsum(
        "uvt,etv->eut",
        shear_flags.reshape(per_dest, src_count, offset_slots),
        selector_two,
        preferred_element_type=jnp.float32,
    )
    flags_two = flags_two.astype(jnp.bfloat16).reshape(src_count, 1, per_dest, 1, offset_slots, 1)
    arrived_two, arrived_flags_two = (
        lax.all_to_all(outgoing_two, "src", split_axis=0, concat_axis=0, tiled=True),
        lax.all_to_all(flags_two, "src", split_axis=0, concat_axis=0, tiled=True),
    )
    midpoint_ids = jnp.arange(src_blocks, dtype=jnp.int32)
    mid_key = (midpoint_ids[:, None] + (src_index - shifts[None, :]) // src_count) % src_blocks
    mid_keys = (
        jnp.arange(src_count, dtype=jnp.int32)[:, None] * per_dest
        + jnp.arange(per_dest, dtype=jnp.int32)[None, :]
    )
    chooser_two = (mid_keys[None, None, :, :] == mid_key[:, :, None, None]).astype(jnp.bfloat16)
    tile_rows = src_blocks * block_edge
    tile_cols = offset_slots * block_edge
    target = jnp.einsum(
        "aruptq,mtau->mprtq", arrived_two, chooser_two, preferred_element_type=jnp.float32
    )
    target = target.reshape(tile_rows, 2 * tile_cols)
    weight = jnp.einsum(
        "aut,mtau->mt",
        arrived_flags_two.reshape(src_count, per_dest, offset_slots),
        chooser_two,
        preferred_element_type=jnp.float32,
    )
    weight = weight * (jnp.abs(offsets) <= band_width[0]).astype(jnp.float32)[None, :]

    def masked(field):
        shaped = (
            field.reshape(src_blocks, block_edge, 2, offset_slots, block_edge)
            * weight[:, None, None, :, None]
        )
        return shaped.reshape(tile_rows, 2 * tile_cols)

    left_full = left_factor.reshape(tile_rows, factor_width)
    right_full = right_factor.reshape(tile_cols, factor_width)
    left_b = left_full.astype(jnp.bfloat16)
    right_b = right_full.astype(jnp.bfloat16)
    residual = masked(times_t(left_b, stacked(right_b)) - target)
    left_count = tile_rows // rcv_count
    right_count = tile_cols // src_count
    for iteration in range(ITERS):
        residual_b = residual.astype(jnp.bfloat16)
        stacked_right = stacked(right_b)
        gradient = lax.psum(
            jnp.dot(residual_b, stacked_right, preferred_element_type=jnp.float32), "rcv"
        )
        own_rows = lax.dynamic_slice_in_dim(gradient, rcv_index * left_count, left_count, 0)
        curvature = masked(times_t(gradient.astype(jnp.bfloat16), stacked_right))
        step_size = left_sums(own_rows, curvature)
        left_full = left_full - step_size * gradient
        left_b = left_full.astype(jnp.bfloat16)
        residual = residual - step_size * curvature
        residual_b = residual.astype(jnp.bfloat16)
        products = lax.dot_general(
            residual_b, left_b, (((0,), (0,)), ((), ())), preferred_element_type=jnp.float32
        )
        gradient_r = lax.psum(combine(products), "src")
        own_rows = lax.dynamic_slice_in_dim(gradient_r, src_index * right_count, right_count, 0)
        curvature = masked(times_t(left_b, stacked(gradient_r.astype(jnp.bfloat16))))
        step_size = right_sums(own_rows, curvature)
        right_full = right_full - step_size * gradient_r
        right_b = right_full.astype(jnp.bfloat16)
        residual = residual - step_size * curvature
    return (left_full.reshape(left_factor.shape), right_full.reshape(right_factor.shape))


def solution(mesh):
    return jax.shard_map(
        per_device,
        mesh=mesh,
        in_specs=(
            P(None, "src", "rcv"),
            P("src", "rcv"),
            P(),
            P(None, "src", None, None),
            P(None, "rcv", None, None),
        ),
        out_specs=(P(None, "src", None, None), P(None, "rcv", None, None)),
        check_vma=False,
    )
```

profile of v0, /device:TPU:1, one launch (start us, length us, event | category | flops | bytes accessed | tf_op | source)
XLA Modules:
  0.0 1015.3 jit_solution(1019897243227720866)
XLA Ops:
  9.0 7.6 all-to-all-start.2
  16.6 22.1 %reshape.360 = bf16[2,32,64,16,64]{4,3,2,1,0:T(8,128)(2,1)} reshape(bf16[2,2048,1024]{2,1,0:T(8,128)(2,1)} %param.5) | data formatting | bytes 16777216 | tf_op jit(solution)/shard_map/reshape | solution.py:70
  38.7 11.5 %convert_bitcast_fusion = bf16[16,2,32,1,64,64]{5,0,4,1,2,3:T(8,128)(2,1)} fusion(bf16[2,32,64,16,64]{4,3,2,1,0:T(8,128)(2,1)} %reshape.360, s32[32,16]{1,0:T(8,128)S(1)} %add_select_fusion), kind=kOutput, calls=%fused_computation.5 | convolution fusion | flops 138420224 | bytes 16779264 | tf_op jit(solution)/shard_map/ripjq,idgj->drigpq/dot_general | solution.py:71
  50.2 15.1 %copy.128 = bf16[16,2,32,1,64,64]{5,4,1,2,3,0:T(8,128)(2,1)} copy(bf16[16,2,32,1,64,64]{5,0,4,1,2,3:T(8,128)(2,1)} %convert_bitcast_fusion) | data formatting | bytes 16777216 | tf_op jit(solution)/shard_map/convert_element_type | solution.py:73
  65.3 19.6 %reshape.382 = bf16[16,2,131072]{2,1,0:T(2,128)(2,1)} reshape(bf16[16,1,32,2,64,64]{5,4,3,2,1,0:T(8,128)(2,1)} %bitcast.116) | data formatting | bytes 16777216
  85.0 6.7 all-to-all-start
  93.3 120.0 %all-to-all-done = bf16[16,2,131072]{2,1,0:T(2,128)(2,1)} async-done(((bf16[16,2,131072]{2,1,0:T(2,128)(2,1)}), bf16[16,2,131072]{2,1,0:T(2,128)(2,1)}, u32[]{:S(2)}, u32[]{:S(2)}) %all-to-all-start) | async-done | bytes 8388640 | tf_op jit(solution)/shard_map/all_to_all | solution.py:79
  213.3 7.7 all-to-all-start.3
  221.0 19.4 %reshape.383 = bf16[16,1,32,2,64,64]{5,4,3,2,1,0:T(8,128)(2,1)} reshape(bf16[16,2,131072]{2,1,0:T(2,128)(2,1)} %all-to-all-done) | data formatting | bytes 16777216
  240.4 18.5 %fusion.7 = bf16[32,6,2,64,64]{4,1,3,2,0:T(8,128)(2,1)} fusion(bf16[16,2,32,1,64,64]{5,4,1,2,3,0:T(8,128)(2,1)} %bitcast.115, s32[32,6]{1,0:T(8,128)S(1)} %copy.63), kind=kOutput, calls=%fused_computation.6 | convolution fusion | flops 51907584 | bytes 11535104 | tf_op jit(solution)/shard_map/brigpq,itbg->riptq/dot_general | solution.py:88
  259.0 10.6 %convert_bitcast_fusion.1 = bf16[8,2,4,64,6,64]{5,0,2,3,1,4:T(8,128)(2,1)S(1)} fusion(bf16[2,4,8,64,6,64]{5,4,3,0,2,1:T(8,128)(2,1)} %bitcast.117, s32[8,6]{0,1:T(8,128)S(1)} %add_select_fusion.3), kind=kOutput, calls=%fused_computation.20 | convolution fusion | flops 26739072 | bytes 6291648 | tf_op jit(solution)/shard_map/ruvptq,etv->eruptq/dot_general | solution.py:106
  269.5 6.3 copy.129
  275.8 9.1 reshape.384
  284.9 4.8 all-to-all-start.1
  292.2 6.2 mul.154
  298.5 12.2 %mul.155 = f32[2048,768]{0,1:T(8,128)} reshape(f32[32,64,2,6,64]{1,0,4,3,2:T(8,128)} %mul.154) | data formatting | bytes 12582912 | tf_op jit(solution)/shard_map/mul | solution.py:143
  310.6 16.7 %all-to-all-done.1 = bf16[8,2,98304]{2,1,0:T(2,128)(2,1)} async-done(((bf16[8,2,98304]{2,1,0:T(2,128)(2,1)}), bf16[8,2,98304]{2,1,0:T(2,128)(2,1)}, u32[]{:S(2)}, u32[]{:S(2)}) %all-to-all-start.1) | async-done | bytes 3145760 | tf_op jit(solution)/shard_map/all_to_all | solution.py:117
  327.4 8.8 reshape.385
  336.2 11.2 %fusion.15 = f32[32,64,2,6,64]{4,0,1,2,3:T(8,128)} fusion(bf16[8,2,4,64,6,64]{5,2,3,1,4,0:T(4,128)(2,1)} %bitcast.118, s32[32,6]{0,1:T(8,128)S(1)} %add_select_fusion.4, s32[8,4]{0,1:T(4,128)S(1)} %iota_add_fusion), kind=kOutput, calls=%fused_computation.21 | convolution fusion | flops 100669440 | bytes 9438080 | tf_op jit(solution)/shard_map/aruptq,mtau->mprtq/dot_general | solution.py:129
  347.4 14.2 %copy.70 = f32[32,64,2,6,64]{1,0,4,3,2:T(8,128)} copy(f32[32,64,2,6,64]{4,0,1,2,3:T(8,128)} %fusion.15) | data formatting | bytes 12582912 | tf_op jit(solution)/shard_map/aruptq,mtau->mprtq/transpose | solution.py:129
  361.5 11.8 %reshape.363 = f32[2048,768]{0,1:T(8,128)} reshape(f32[32,64,2,6,64]{1,0,4,3,2:T(8,128)} %copy.70) | data formatting | bytes 12582912 | tf_op jit(solution)/shard_map/reshape | solution.py:132
  373.3 5.6 fusion.10
  379.0 2.7 copy-done
  381.6 2.4 fusion.26
  384.1 87.7 %all-reduce.9.cloned.1.call-done = f32[2048,256]{1,0:T(8,128)} async-done(((f32[2048,256]{1,0:T(8,128)}), f32[2048,256]{1,0:T(8,128)}) %all-reduce.9.cloned.1.call-update) | async-done | bytes 2097168 | tf_op jit(solution)/shard_map/psum | solution.py:158
  471.7 8.6 multiply_reduce_fusion.3
  480.9 65.8 %all-reduce.3 = (f32[]{:T(128)}, f32[]{:T(128)}) all-reduce(f32[]{:T(128)} %multiply_reduce_fusion.7, f32[]{:T(128)} %get-tuple-element.32), channel_id=1, replica_groups=mesh['src'=8,'rcv'=16] {'src','rcv'}, use_global_device_ids=true, to_apply=%region_2.3 | all-reduce | flops 2 | bytes 16 | tf_op jit(solution)/shard_map/psum | solution.py:37
  548.0 1.9 fusion.31
  549.9 5.8 fusion.24
  556.8 54.9 %all-reduce.11.cloned.1.call-done = f32[384,256]{0,1:T(8,128)} async-done(((f32[384,256]{0,1:T(8,128)}), f32[384,256]{0,1:T(8,128)}) %all-reduce.11.cloned.1.call-update) | async-done | bytes 393232 | tf_op jit(solution)/shard_map/psum | solution.py:171
  611.7 1.0 convert_element_type.113
  612.8 7.1 multiply_reduce_fusion.2
  620.6 67.1 %all-reduce.2 = (f32[]{:T(128)}, f32[]{:T(128)}) all-reduce(f32[]{:T(128)} %multiply_reduce_fusion.6, f32[]{:T(128)} %get-tuple-element.34), channel_id=1, replica_groups=mesh['src'=8,'rcv'=16] {'src','rcv'}, use_global_device_ids=true, to_apply=%region_7.8 | all-reduce | flops 2 | bytes 16 | tf_op jit(solution)/shard_map/psum | solution.py:44
  689.8 8.6 multiply_subtract_fusion
  698.4 2.7 copy-done.1
  701.0 3.4 fusion.22
  704.5 85.6 %all-reduce.13.cloned.1.call-done = f32[2048,256]{1,0:T(8,128)} async-done(((f32[2048,256]{1,0:T(8,128)}), f32[2048,256]{1,0:T(8,128)}) %all-reduce.13.cloned.1.call-update) | async-done | bytes 2097168 | tf_op jit(solution)/shard_map/psum | solution.py:158
  790.2 7.8 multiply_reduce_fusion.1
  798.0 1.5 multiply_reduce_fusion.5
  799.5 65.8 %all-reduce.1 = (f32[]{:T(128)}, f32[]{:T(128)}) all-reduce(f32[]{:T(128)} %multiply_reduce_fusion.5, f32[]{:T(128)} %get-tuple-element.36), channel_id=1, replica_groups=mesh['src'=8,'rcv'=16] {'src','rcv'}, use_global_device_ids=true, to_apply=%region_12.13 | all-reduce | flops 2 | bytes 16 | tf_op jit(solution)/shard_map/psum | solution.py:37
  866.7 2.8 multiply_subtract_fusion.3
  869.5 1.8 copy-done.4
  871.3 4.1 fusion.20
  876.3 55.2 %all-reduce.15.cloned.1.call-done = f32[384,256]{0,1:T(8,128)} async-done(((f32[384,256]{0,1:T(8,128)}), f32[384,256]{0,1:T(8,128)}) %all-reduce.15.cloned.1.call-update) | async-done | bytes 393232 | tf_op jit(solution)/shard_map/psum | solution.py:171
  931.5 1.1 convert_element_type.119
  932.6 5.9 multiply_reduce_fusion
  939.2 67.1 %all-reduce = (f32[]{:T(128)}, f32[]{:T(128)}) all-reduce(f32[]{:T(128)} %multiply_reduce_fusion.4, f32[]{:T(128)} %multiply_reduce_fusion), channel_id=1, replica_groups=mesh['src'=8,'rcv'=16] {'src','rcv'}, use_global_device_ids=true, to_apply=%region_17.18 | all-reduce | flops 2 | bytes 16 | tf_op jit(solution)/shard_map/psum | solution.py:44
  1007.6 0.9 copy.78
  (78 shorter events, 10.3 us)
Async XLA Ops:
  9.0 76.0 %all-to-all-start.2 = ((bf16[16,1,32,1,1,1]{2,5,4,3,1,0:T(2,128)(2,1)}), bf16[16,1,32,1,1,1]{2,5,4,3,1,0:T(2,128)(2,1)S(1)}, u32[]{:S(2)}, u32[]{:S(2)}) async-start(bf16[16,1,32,1,1,1]{2,5,4,3,1,0:T(2,128)(2,1)} %copy.71), calls=%async_computation.2 | async-start | bytes 16384 | tf_op jit(solution)/shard_map/all_to_all | solution.py:80
  85.0 128.3 %all-to-all-start = ((bf16[16,2,131072]{2,1,0:T(2,128)(2,1)}), bf16[16,2,131072]{2,1,0:T(2,128)(2,1)}, u32[]{:S(2)}, u32[]{:S(2)}) async-start(bf16[16,2,131072]{2,1,0:T(2,128)(2,1)} %reshape.382), calls=%async_computation | async-start | bytes 16777216 | tf_op jit(solution)/shard_map/all_to_all | solution.py:79
  213.3 71.6 %all-to-all-start.3 = ((bf16[8,1,4,1,6,1]{4,2,5,3,1,0:T(4,128)(2,1)}), bf16[8,1,4,1,6,1]{4,2,5,3,1,0:T(4,128)(2,1)S(1)}, u32[]{:S(2)}, u32[]{:S(2)}) async-start(bf16[8,1,4,1,6,1]{4,2,5,3,1,0:T(4,128)(2,1)} %copy.72), calls=%async_computation.3 | async-start | bytes 16384 | tf_op jit(solution)/shard_map/all_to_all | solution.py:118
  275.8 15.2 %copy-start.12 = (f32[6,1,64,256]{3,2,1,0:T(8,128)S(1)}, f32[6,1,64,256]{3,2,1,0:T(8,128)}, u32[]{:S(2)}) copy-start(f32[6,1,64,256]{3,2,1,0:T(8,128)} %param.9) | copy-start | bytes 1179652
  275.8 15.2 %copy-start.6 = (f32[32,1,64,256]{3,2,1,0:T(8,128)S(1)}, f32[32,1,64,256]{3,2,1,0:T(8,128)}, u32[]{:S(2)}) copy-start(f32[32,1,64,256]{3,2,1,0:T(8,128)} %param.8) | copy-start | bytes 6291460
  284.9 42.5 %all-to-all-start.1 = ((bf16[8,2,98304]{2,1,0:T(2,128)(2,1)}), bf16[8,2,98304]{2,1,0:T(2,128)(2,1)}, u32[]{:S(2)}, u32[]{:S(2)}) async-start(bf16[8,2,98304]{2,1,0:T(2,128)(2,1)} %reshape.384), calls=%async_computation.1 | async-start | bytes 6291456 | tf_op jit(solution)/shard_map/all_to_all | solution.py:117
  289.7 182.0 %all-reduce.9.cloned.1.call-start = ((), (), s32[]{:S(2)}) async-start(), calls=%async_computation.4 | async-start | bytes 4194304 | tf_op jit(solution)/shard_map/psum | solution.py:158
  379.0 2.7 copy-start
  384.0 227.7 %all-reduce.11.cloned.1.call-start = ((), (), s32[]{:S(2)}) async-start(), calls=%async_computation.5 | async-start | bytes 786432 | tf_op jit(solution)/shard_map/psum | solution.py:171
  471.7 8.6 copy-start.2
  549.9 6.7 copy-start.13
  556.5 233.6 %all-reduce.13.cloned.1.call-start = ((), (), s32[]{:S(2)}) async-start(), calls=%async_computation.6 | async-start | bytes 4194304 | tf_op jit(solution)/shard_map/psum | solution.py:158
  556.8 132.2 %copy-start.8 = (f32[384,256]{0,1:T(8,128)}, f32[384,256]{0,1:T(8,128)S(1)}, u32[]{:S(2)}) copy-start(f32[384,256]{0,1:T(8,128)S(1)} %copy.75) | copy-start | bytes 1179652
  612.8 7.1 copy-start.7
  689.0 0.7 copy-start.10
  698.4 2.7 copy-start.1
  704.5 162.2 %copy-start.3 = (f32[2048,256]{1,0:T(8,128)S(1)}, f32[2048,256]{1,0:T(8,128)}, u32[]{:S(2)}) copy-start(f32[2048,256]{1,0:T(8,128)} %all-reduce.9.cloned.1.call-done) | copy-start | bytes 6291460
  704.5 227.0 %all-reduce.15.cloned.1.call-start = ((), (), s32[]{:S(2)}) async-start(), calls=%async_computation.7 | async-start | bytes 786432 | tf_op jit(solution)/shard_map/psum | solution.py:171
  866.6 4.6 copy-start.4
  869.5 6.0 copy-start.5
  875.4 132.1 %copy-start.9 = (f32[384,256]{0,1:T(8,128)S(1)}, f32[384,256]{0,1:T(8,128)}, u32[]{:S(2)}) copy-start(f32[384,256]{0,1:T(8,128)} %copy-done.8) | copy-start | bytes 1179652
  931.5 7.0 copy-start.11
Sparse Core Ops, SparseCore 0:
  384.1 87.5 all-reduce.8
  556.7 54.9 all-reduce.10
  704.6 85.5 all-reduce.12
  876.4 54.9 all-reduce.14
where the time goes:
time: 1020 us
  waiting for transfers between devices  420 us (41%)
  blocking collectives  266 us (26%)
  local copies, waits for them, and re-layouts  155 us (15%)
  matrix products  103 us (10%)
  starting transfers between devices  26.9 us (3%)
  other arithmetic  24.4 us (2%)
  between operations  20.2 us (2%)
    psum x2, waiting for transfers between devices, per_device(): lax.psum(jnp.dot(residual_b, stacked_right, preferred_element_type=jnp.fl...  173 us
    psum x2, blocking collectives, right_sums(): lax.psum((jnp.sum(own_rows * own_rows), jnp.sum(curvature * curvature)),...  134 us
    psum x2, blocking collectives, left_sums(): lax.psum((jnp.sum(own_rows * own_rows), jnp.sum(curvature * curvature)),...  132 us
    all_to_all x1, waiting for transfers between devices, per_device(): lax.all_to_all(outgoing, 'rcv', split_axis=0, concat_axis=0, tiled=True)  120 us
    psum x2, waiting for transfers between devices, per_device(): gradient_r = lax.psum(combine(products), 'src')  110 us
    unnamed x34, local copies, waits for them, and re-layouts  64.3 us
    dot_general x5, matrix products, times_t(): lax.dot_general(first, second, (((1,), (1,)), ((), ())), preferred_elemen...  35 us
    reshape x1, local copies, waits for them, and re-layouts, per_device(): blocked = data.reshape(2, src_blocks, block_edge, rcv_blocks, block_edge)  22.1 us
  transfers between devices with their start and end apart: 8, of which 6 were waited for; matrix products, arithmetic and copies ran while one was open for 15% of the time, Pallas kernels for 0%

commit v1 on v0

--- a/solution.py
+++ b/solution.py
@@ -155,8 +155,11 @@
     for iteration in range(ITERS):
         residual_b = residual.astype(jnp.bfloat16)
         stacked_right = stacked(right_b)
-        gradient = lax.psum(
-            jnp.dot(residual_b, stacked_right, preferred_element_type=jnp.float32), "rcv"
+        gradient = jnp.sum(
+            lax.all_gather(
+                jnp.dot(residual_b, stacked_right, preferred_element_type=jnp.float32), "rcv"
+            ),
+            axis=0,
         )
         own_rows = lax.dynamic_slice_in_dim(gradient, rcv_index * left_count, left_count, 0)
         curvature = masked(times_t(gradient.astype(jnp.bfloat16), stacked_right))

time: 1020 us -> 1300 us (1.27)
  waiting for transfers between devices: 420 us -> 631 us
  other arithmetic: 24.4 us -> 62.7 us
  local copies, waits for them, and re-layouts: 155 us -> 180 us
    all_gather x0 -> x2, waiting for transfers between devices: none -> 389 us  [per_device(): lax.all_gather(jnp.dot(residual_b, stacked_right, preferred_element_type=...]
    psum x2 -> x0, waiting for transfers between devices: 173 us -> none  [per_device(): lax.psum(jnp.dot(residual_b, stacked_right, preferred_element_type=jnp.fl...]
    mul x0 -> x2, local copies, waits for them, and re-layouts: none -> 25.1 us  [per_device(): residual = residual - step_size * curvature]
    reduce_sum x0 -> x2, other arithmetic: none -> 24.2 us  [per_device(): jnp.sum(lax.all_gather(jnp.dot(residual_b, stacked_right, preferred_eleme...]
    unnamed x34 -> x52, local copies, waits for them, and re-layouts: 64.3 us -> 62.3 us
  transfers between devices with their start and end apart: 8 -> 8, of which waited for: 6 -> 6; matrix products, arithmetic and copies ran while one was open for 15% -> 12% of each run, Pallas kernels for 0% -> 0%
where the time goes in v1:
time: 1300 us; the launch traced here: 1290 us
  waiting for transfers between devices  631 us (49%)
  blocking collectives  264 us (20%)
  local copies, waits for them, and re-layouts  180 us (14%)
  matrix products  102 us (8%)
  other arithmetic  62.7 us (5%)
  starting transfers between devices  26.9 us (2%)
  between operations  20.4 us (2%)
    all_gather x2, waiting for transfers between devices, per_device(): lax.all_gather(jnp.dot(residual_b, stacked_right, preferred_element_type=...  389 us
    psum x2, blocking collectives, right_sums(): lax.psum((jnp.sum(own_rows * own_rows), jnp.sum(curvature * curvature)),...  134 us
    psum x2, blocking collectives, left_sums(): lax.psum((jnp.sum(own_rows * own_rows), jnp.sum(curvature * curvature)),...  130 us
    all_to_all x1, waiting for transfers between devices, per_device(): lax.all_to_all(outgoing, 'rcv', split_axis=0, concat_axis=0, tiled=True)  120 us
    psum x2, waiting for transfers between devices, per_device(): gradient_r = lax.psum(combine(products), 'src')  105 us
    unnamed x52, local copies, waits for them, and re-layouts  62.3 us
    dot_general x5, matrix products, times_t(): lax.dot_general(first, second, (((1,), (1,)), ((), ())), preferred_elemen...  34.5 us
  transfers between devices with their start and end apart: 8, of which 6 were waited for; matrix products, arithmetic and copies ran while one was open for 12% of the time, Pallas kernels for 0%

profile of v1, /device:TPU:1, one launch (start us, length us, event | category | flops | bytes accessed | tf_op | source)
XLA Modules:
  0.0 1287.7 jit_solution(17860866169734825036)
XLA Ops:
  9.0 7.6 all-to-all-start.2
  16.6 22.1 %reshape.396 = bf16[2,32,64,16,64]{4,3,2,1,0:T(8,128)(2,1)} reshape(bf16[2,2048,1024]{2,1,0:T(8,128)(2,1)} %param.5) | data formatting | bytes 16777216 | tf_op jit(solution)/shard_map/reshape | solution.py:70
  38.7 11.5 convert_bitcast_fusion
  50.2 15.1 %copy.140 = bf16[16,2,32,1,64,64]{5,4,1,2,3,0:T(8,128)(2,1)} copy(bf16[16,2,32,1,64,64]{5,0,4,1,2,3:T(8,128)(2,1)} %convert_bitcast_fusion) | data formatting | bytes 16777216 | tf_op jit(solution)/shard_map/convert_element_type | solution.py:73
  65.3 19.6 %reshape.423 = bf16[16,2,131072]{2,1,0:T(2,128)(2,1)} reshape(bf16[16,1,32,2,64,64]{5,4,3,2,1,0:T(8,128)(2,1)} %bitcast.139) | data formatting | bytes 16777216
  85.0 6.7 all-to-all-start
  93.3 120.0 %all-to-all-done = bf16[16,2,131072]{2,1,0:T(2,128)(2,1)} async-done(((bf16[16,2,131072]{2,1,0:T(2,128)(2,1)}), bf16[16,2,131072]{2,1,0:T(2,128)(2,1)}, u32[]{:S(2)}, u32[]{:S(2)}) %all-to-all-start) | async-done | bytes 8388640 | tf_op jit(solution)/shard_map/all_to_all | solution.py:79
  213.3 7.7 all-to-all-start.3
  221.0 19.5 %reshape.424 = bf16[16,1,32,2,64,64]{5,4,3,2,1,0:T(8,128)(2,1)} reshape(bf16[16,2,131072]{2,1,0:T(2,128)(2,1)} %all-to-all-done) | data formatting | bytes 16777216
  240.5 18.5 %fusion.7 = bf16[32,6,2,64,64]{4,1,3,2,0:T(8,128)(2,1)} fusion(bf16[16,2,32,1,64,64]{5,4,1,2,3,0:T(8,128)(2,1)} %bitcast.138, s32[32,6]{1,0:T(8,128)S(1)} %copy.67), kind=kOutput, calls=%fused_computation.9 | convolution fusion | flops 51907584 | bytes 11535104 | tf_op jit(solution)/shard_map/brigpq,itbg->riptq/dot_general | solution.py:88
  259.0 10.8 convert_bitcast_fusion.1
  269.8 6.3 copy.141
  276.0 9.1 reshape.425
  285.1 4.8 all-to-all-start.1
  292.7 6.2 mul.183.clone
  298.9 11.9 mul.184
  310.9 16.7 %all-to-all-done.1 = bf16[8,2,98304]{2,1,0:T(2,128)(2,1)} async-done(((bf16[8,2,98304]{2,1,0:T(2,128)(2,1)}), bf16[8,2,98304]{2,1,0:T(2,128)(2,1)}, u32[]{:S(2)}, u32[]{:S(2)}) %all-to-all-start.1) | async-done | bytes 3145760 | tf_op jit(solution)/shard_map/all_to_all | solution.py:117
  327.6 8.8 reshape.426
  336.4 11.2 fusion.15
  347.6 14.2 %copy.74 = f32[32,64,2,6,64]{1,0,4,3,2:T(8,128)} copy(f32[32,64,2,6,64]{4,0,1,2,3:T(8,128)} %fusion.15) | data formatting | bytes 12582912 | tf_op jit(solution)/shard_map/aruptq,mtau->mprtq/transpose | solution.py:129
  361.7 11.8 reshape.399
  373.5 5.6 fusion.10
  379.2 2.6 copy-done
  381.8 2.4 fusion.26
  384.2 195.6 %all-gather.5.cloned.1.call-done = f32[32768,256]{1,0:T(8,128)} async-done(((f32[2048,256]{1,0:T(8,128)}), f32[32768,256]{1,0:T(8,128)}) %all-gather.5.cloned.1.call-update) | async-done | bytes 33554448 | tf_op jit(solution)/shard_map/all_gather | solution.py:159
  579.9 12.1 reduce_sum.90
  591.9 7.8 multiply_reduce_fusion.3
  600.4 65.1 %all-reduce.3 = (f32[]{:T(128)}, f32[]{:T(128)}) all-reduce(f32[]{:T(128)} %multiply_reduce_fusion.7, f32[]{:T(128)} %get-tuple-element.34), channel_id=1, replica_groups=mesh['src'=8,'rcv'=16] {'src','rcv'}, use_global_device_ids=true, to_apply=%region_2.3 | all-reduce | flops 2 | bytes 16 | tf_op jit(solution)/shard_map/psum | solution.py:37
  666.8 3.4 bitcast_subtract_fusion.1
  671.0 4.3 fusion.24
  677.1 3.2 sub.101
  680.3 51.8 %all-reduce.7.cloned.1.call-done = f32[384,256]{0,1:T(8,128)} async-done(((f32[384,256]{0,1:T(8,128)}), f32[384,256]{0,1:T(8,128)}) %all-reduce.7.cloned.1.call-update) | async-done | bytes 393232 | tf_op jit(solution)/shard_map/psum | solution.py:174
  733.4 8.6 multiply_reduce_fusion.1
  742.8 67.1 %all-reduce.2 = (f32[]{:T(128)}, f32[]{:T(128)}) all-reduce(f32[]{:T(128)} %multiply_reduce_fusion.6, f32[]{:T(128)} %get-tuple-element.36), channel_id=1, replica_groups=mesh['src'=8,'rcv'=16] {'src','rcv'}, use_global_device_ids=true, to_apply=%region_7.8 | all-reduce | flops 2 | bytes 16 | tf_op jit(solution)/shard_map/psum | solution.py:44
  811.2 10.1 multiply_multiply_fusion
  821.3 13.3 %copy.80 = f32[32,64,2,6,64]{1,0,4,3,2:T(8,128)} copy(f32[32,64,2,6,64]{4,1,3,2,0:T(8,128)} %multiply_multiply_fusion) | data formatting | bytes 12582912 | tf_op jit(solution)/shard_map/mul | solution.py:180
  834.6 11.8 mul.201
  846.4 8.7 fusion.28
  857.9 2.4 fusion.22
  860.4 193.6 %all-gather.7.cloned.1.call-done = f32[32768,256]{1,0:T(8,128)} async-done(((f32[2048,256]{1,0:T(8,128)}), f32[32768,256]{1,0:T(8,128)}) %all-gather.7.cloned.1.call-update) | async-done | bytes 33554448 | tf_op jit(solution)/shard_map/all_gather | solution.py:159
  1054.0 12.1 reduce_sum.95
  1066.8 7.0 multiply_reduce_fusion.2
  1073.8 65.1 %all-reduce.1 = (f32[]{:T(128)}, f32[]{:T(128)}) all-reduce(f32[]{:T(128)} %multiply_reduce_fusion.5, f32[]{:T(128)} %get-tuple-element.38), channel_id=1, replica_groups=mesh['src'=8,'rcv'=16] {'src','rcv'}, use_global_device_ids=true, to_apply=%region_12.13 | all-reduce | flops 2 | bytes 16 | tf_op jit(solution)/shard_map/psum | solution.py:37
  1140.2 6.4 fusion.20
  1147.6 1.9 sub.107
  1149.6 53.7 %all-reduce.9.cloned.1.call-done = f32[384,256]{0,1:T(8,128)} async-done(((f32[384,256]{0,1:T(8,128)}), f32[384,256]{0,1:T(8,128)}) %all-reduce.9.cloned.1.call-update) | async-done | bytes 393232 | tf_op jit(solution)/shard_map/psum | solution.py:174
  1205.3 5.4 multiply_reduce_fusion
  1211.3 67.1 %all-reduce = (f32[]{:T(128)}, f32[]{:T(128)}) all-reduce(f32[]{:T(128)} %multiply_reduce_fusion.4, f32[]{:T(128)} %multiply_reduce_fusion), channel_id=1, replica_groups=mesh['src'=8,'rcv'=16] {'src','rcv'}, use_global_device_ids=true, to_apply=%region_17.18 | all-reduce | flops 2 | bytes 16 | tf_op jit(solution)/shard_map/psum | solution.py:44
  (108 shorter events, 19.0 us)
Async XLA Ops:
  9.0 76.0 %all-to-all-start.2 = ((bf16[16,1,32,1,1,1]{2,5,4,3,1,0:T(2,128)(2,1)}), bf16[16,1,32,1,1,1]{2,5,4,3,1,0:T(2,128)(2,1)S(1)}, u32[]{:S(2)}, u32[]{:S(2)}) async-start(bf16[16,1,32,1,1,1]{2,5,4,3,1,0:T(2,128)(2,1)} %copy.75), calls=%async_computation.2 | async-start | bytes 16384 | tf_op jit(solution)/shard_map/all_to_all | solution.py:80
  85.0 128.3 %all-to-all-start = ((bf16[16,2,131072]{2,1,0:T(2,128)(2,1)}), bf16[16,2,131072]{2,1,0:T(2,128)(2,1)}, u32[]{:S(2)}, u32[]{:S(2)}) async-start(bf16[16,2,131072]{2,1,0:T(2,128)(2,1)} %reshape.423), calls=%async_computation | async-start | bytes 16777216 | tf_op jit(solution)/shard_map/all_to_all | solution.py:79
  213.3 71.8 %all-to-all-start.3 = ((bf16[8,1,4,1,6,1]{4,2,5,3,1,0:T(4,128)(2,1)}), bf16[8,1,4,1,6,1]{4,2,5,3,1,0:T(4,128)(2,1)S(1)}, u32[]{:S(2)}, u32[]{:S(2)}) async-start(bf16[8,1,4,1,6,1]{4,2,5,3,1,0:T(4,128)(2,1)} %copy.76), calls=%async_computation.3 | async-start | bytes 16384 | tf_op jit(solution)/shard_map/all_to_all | solution.py:118
  276.0 15.3 %copy-start.12 = (f32[6,1,64,256]{3,2,1,0:T(8,128)S(1)}, f32[6,1,64,256]{3,2,1,0:T(8,128)}, u32[]{:S(2)}) copy-start(f32[6,1,64,256]{3,2,1,0:T(8,128)} %param.9) | copy-start | bytes 1179652
  276.0 15.3 %copy-start.4 = (f32[32,1,64,256]{3,2,1,0:T(8,128)S(1)}, f32[32,1,64,256]{3,2,1,0:T(8,128)}, u32[]{:S(2)}) copy-start(f32[32,1,64,256]{3,2,1,0:T(8,128)} %param.8) | copy-start | bytes 6291460
  285.1 42.5 %all-to-all-start.1 = ((bf16[8,2,98304]{2,1,0:T(2,128)(2,1)}), bf16[8,2,98304]{2,1,0:T(2,128)(2,1)}, u32[]{:S(2)}, u32[]{:S(2)}) async-start(bf16[8,2,98304]{2,1,0:T(2,128)(2,1)} %reshape.425), calls=%async_computation.1 | async-start | bytes 6291456 | tf_op jit(solution)/shard_map/all_to_all | solution.py:117
  289.9 290.0 %all-gather.5.cloned.1.call-start = ((), (), s32[]{:S(2)}) async-start(), calls=%async_computation.6 | async-start | bytes 35651584 | tf_op jit(solution)/shard_map/all_gather | solution.py:159
  291.2 0.6 copy-start.20
  291.3 0.6 copy-start.18
  310.8 25.5 %copy-start.19 = (s32[32,6]{0,1:T(8,128)S(1)}, s32[32,6]{0,1:T(8,128)}, u32[]{:S(2)}) copy-start(s32[32,6]{0,1:T(8,128)} %copy-done.18) | copy-start | bytes 2308
  310.9 25.5 %copy-start.21 = (s32[8,4]{0,1:T(4,128)S(1)}, s32[8,4]{0,1:T(4,128)}, u32[]{:S(2)}) copy-start(s32[8,4]{0,1:T(4,128)} %copy-done.20) | copy-start | bytes 388
  379.1 2.6 copy-start
  384.2 347.9 %all-reduce.7.cloned.1.call-start = ((), (), s32[]{:S(2)}) async-start(), calls=%async_computation.4 | async-start | bytes 786432 | tf_op jit(solution)/shard_map/psum | solution.py:174
  666.8 4.2 copy-start.1
  670.3 5.0 copy-start.3
  671.0 5.2 copy-start.13
  671.0 6.1 copy-start.5
  676.1 377.8 %all-gather.7.cloned.1.call-start = ((), (), s32[]{:S(2)}) async-start(), calls=%async_computation.7 | async-start | bytes 35651584 | tf_op jit(solution)/shard_map/all_gather | solution.py:159
  733.4 8.6 copy-start.6
  855.1 2.6 copy-start.2
  856.4 1.4 copy-start.8
  856.5 1.4 copy-start.14
  856.5 1.4 copy-start.16
  860.3 342.9 %all-reduce.9.cloned.1.call-start = ((), (), s32[]{:S(2)}) async-start(), calls=%async_computation.5 | async-start | bytes 786432 | tf_op jit(solution)/shard_map/psum | solution.py:174
  1054.0 12.8 copy-start.9
  1054.0 12.8 copy-start.15
  1054.0 12.8 copy-start.17
  1149.5 61.1 %copy-start.11 = (f32[32,1,64,256]{3,2,1,0:T(8,128)}, f32[32,1,64,256]{3,2,1,0:T(8,128)S(1)}, u32[]{:S(2)}) copy-start(f32[32,1,64,256]{3,2,1,0:T(8,128)S(1)} %sub.107) | copy-start | bytes 6291460
  1205.2 5.4 copy-start.10
  1205.3 74.5 %copy-start.7 = (f32[384,256]{0,1:T(8,128)S(1)}, f32[384,256]{0,1:T(8,128)}, u32[]{:S(2)}) copy-start(f32[384,256]{0,1:T(8,128)} %copy.81) | copy-start | bytes 1179652
Sparse Core Ops, SparseCore 0:
  384.3 195.5 all-gather.4
  676.3 55.7 all-reduce.6
  860.4 193.5 all-gather.6
  1147.6 55.5 all-reduce.8
